TPU v7x, 32 devices: a whole 2x2x4 slice. The times are simulated.
32 devices in a mesh: fsdp: 8 (over z, x), ctx: 2 (over core), tp: 2 (over y).
Axes of the slice: x: 2, y: 2, z: 4, core: 2. Of those that a mesh axis runs over, the one named last changes fastest.
Arguments:
- inputs: bfloat16 [8, 320, 1024], P('fsdp', 'ctx'), may hold values from -11 to 11, as said below
- lengths: int32 [8], P('fsdp'), may hold values from 224 to 320, as said below
- grad_out: bfloat16 [8, 320, 1024], P('fsdp', 'ctx'), may hold values from -6 to 6
- ln1_gain: bfloat16 [1024], P(('fsdp', 'ctx')), may hold values from 0.099609375 to 1.8984375
- ln1_shift: bfloat16 [1024], P(('fsdp', 'ctx')), may hold values from -3 to 3
- w_qkv: bfloat16 [1024, 3, 1024], P(('fsdp', 'ctx'), None, 'tp'), may hold values from -0.1875 to 0.1875
- b_qv: bfloat16 [1024, 2], P(('fsdp', 'ctx'), 'tp'), may hold values from -3 to 3
- w_proj: bfloat16 [1024, 1024], P(('fsdp', 'ctx'), 'tp'), may hold values from -0.5 to 0.5
- b_proj: bfloat16 [1024], P(('fsdp', 'ctx')), may hold values from -3 to 3
- ln2_gain: bfloat16 [1024], P(('fsdp', 'ctx')), may hold values from 0.099609375 to 1.8984375
- ln2_shift: bfloat16 [1024], P(('fsdp', 'ctx')), may hold values from -3 to 3
- w_up: bfloat16 [1024, 4096], P(('fsdp', 'ctx'), 'tp'), may hold values from -0.1875 to 0.1875
- b_up: bfloat16 [2048, 2], P(('fsdp', 'ctx'), 'tp'), may hold values from -3 to 3
- w_down: bfloat16 [1024, 4096], P(('fsdp', 'ctx'), 'tp'), may hold values from -0.09375 to 0.09375
- b_down: bfloat16 [1024], P(('fsdp', 'ctx')), may hold values from -3 to 3
Outputs:
- output: bfloat16 [8, 320, 1024], P('fsdp', 'ctx')
- grad_inputs: float32 [8, 320, 1024], P('fsdp', 'ctx')
- grad_ln1_gain: float32 [1024], P(('fsdp', 'ctx'))
- grad_ln1_shift: float32 [1024], P(('fsdp', 'ctx'))
- grad_w_qkv: float32 [1024, 3, 1024], P(('fsdp', 'ctx'), None, 'tp')
- grad_b_qv: float32 [1024, 2], P(('fsdp', 'ctx'), 'tp')
- grad_w_proj: float32 [1024, 1024], P(('fsdp', 'ctx'), 'tp')
- grad_b_proj: float32 [1024], P(('fsdp', 'ctx'))
- grad_ln2_gain: float32 [1024], P(('fsdp', 'ctx'))
- grad_ln2_shift: float32 [1024], P(('fsdp', 'ctx'))
- grad_w_up: float32 [1024, 4096], P(('fsdp', 'ctx'), 'tp')
- grad_b_up: float32 [2048, 2], P(('fsdp', 'ctx'), 'tp')
- grad_w_down: float32 [1024, 4096], P(('fsdp', 'ctx'), 'tp')
- grad_b_down: float32 [1024], P(('fsdp', 'ctx'))
- rms: float32 [5], replicated
Inputs may be any that keep to these rules, and one draw needn't show every extreme that they name: The lengths 320 and 224 both occur in every draw. `inputs`: rows at or past an image's length are never read.
All inputs are finite; a program needn't handle non-finite values.
Results may differ from a plain program's by a relative error of at most 0.014.
Values may be sent and summed in bfloat16 or wider, within the bound.
No kernel may reach another device: no remote copies, remote signals or barrier semaphores. Data moves between devices by JAX's collectives and lax.ppermute only.
A program may use at most 128 MiB of HBM per device.

v0:
```python
from functools import partial
import jax
import jax.numpy as jnp
from jax import lax
from jax.sharding import PartitionSpec as P

D = 1024
HD = 64
EPSILON = 1e-06
MASK_FILL = -1e30


def layer_norm(values_in, gain, shift):
    mean_val = jnp.mean(values_in, axis=-1, keepdims=True)
    centered = values_in - mean_val
    spread = jnp.mean(centered * centered, axis=-1, keepdims=True)
    return centered * lax.rsqrt(spread + EPSILON) * gain + shift


def contract(left, right, left_dim, right_dim):
    return lax.dot_general(
        left, right, (((left_dim,), (right_dim,)), ((), ())), preferred_element_type=jnp.float32
    )


def attn_scores(query_heads, key_all, key_valid):
    scores = jnp.einsum(
        "bqhd,bkhd->bhqk", query_heads, key_all, preferred_element_type=jnp.float32
    ) * HD ** (-0.5)
    return jnp.where(key_valid[:, None, None, :], scores, MASK_FILL)


def body(
    inputs,
    lengths,
    grad_out,
    ln1_gain,
    ln1_shift,
    w_qkv,
    b_qv,
    w_proj,
    b_proj,
    ln2_gain,
    ln2_shift,
    w_up,
    b_up,
    w_down,
    b_down,
):
    gathered = (
        lax.all_gather(ln1_gain, ("fsdp", "ctx"), axis=0, tiled=True),
        lax.all_gather(ln1_shift, ("fsdp", "ctx"), axis=0, tiled=True),
        lax.all_gather(w_qkv, ("fsdp", "ctx"), axis=0, tiled=True),
        lax.all_gather(b_qv, ("fsdp", "ctx"), axis=0, tiled=True),
        lax.all_gather(w_proj, ("fsdp", "ctx"), axis=0, tiled=True),
        lax.all_gather(b_proj, ("fsdp", "ctx"), axis=0, tiled=True),
        lax.all_gather(ln2_gain, ("fsdp", "ctx"), axis=0, tiled=True),
        lax.all_gather(ln2_shift, ("fsdp", "ctx"), axis=0, tiled=True),
        lax.all_gather(w_up, ("fsdp", "ctx"), axis=0, tiled=True),
        lax.all_gather(b_up, ("fsdp", "ctx"), axis=0, tiled=True),
        lax.all_gather(w_down, ("fsdp", "ctx"), axis=0, tiled=True),
        lax.all_gather(b_down, ("fsdp", "ctx"), axis=0, tiled=True),
    )
    (
        gain_first,
        shift_first,
        qkv_full,
        qv_bias,
        proj_full,
        proj_bias,
        gain_second,
        shift_second,
        up_full,
        up_bias,
        down_full,
        down_bias,
    ) = gathered
    images, half_slots = (inputs.shape[0], inputs.shape[1])
    row_count = images * half_slots
    slot_total = half_slots * lax.axis_size("ctx")
    slot_ids = lax.axis_index("ctx") * half_slots + jnp.arange(half_slots, dtype=jnp.int32)
    is_valid = (slot_ids[None, :] < lengths[:, None]).astype(jnp.float32)
    key_valid = jnp.arange(slot_total, dtype=jnp.int32)[None, :] < lengths[:, None]
    row_valid = is_valid.reshape(row_count, 1)
    gain_one = gain_first.astype(jnp.float32)
    shift_one = shift_first.astype(jnp.float32)
    gain_two = gain_second.astype(jnp.float32)
    shift_two = shift_second.astype(jnp.float32)
    entering = inputs.astype(jnp.float32).reshape(row_count, D) * row_valid
    normed = layer_norm(entering, gain_one, shift_one).astype(jnp.bfloat16)
    local_width = qkv_full.shape[2]
    local_heads = local_width // HD
    qkv_flat = qkv_full.reshape(D, 3 * local_width)
    packed = jnp.dot(normed, qkv_flat, preferred_element_type=jnp.float32).reshape(
        row_count, 3, local_width
    )
    bias_values = qv_bias.astype(jnp.float32)[:, 0]
    query_part = (packed[:, 0] + bias_values[:local_width]).astype(jnp.bfloat16)
    key_part = packed[:, 1].astype(jnp.bfloat16)
    value_part = (packed[:, 2] + bias_values[local_width:]).astype(jnp.bfloat16)
    head_shape = (images, half_slots, local_heads, HD)
    query_heads = query_part.reshape(head_shape)
    key_all, value_all = (
        lax.all_gather(key_part.reshape(head_shape), "ctx", axis=1, tiled=True),
        lax.all_gather(value_part.reshape(head_shape), "ctx", axis=1, tiled=True),
    )
    scores = attn_scores(query_heads, key_all, key_valid)
    row_max = jnp.max(scores, axis=-1, keepdims=True)
    raised = jnp.exp(scores - row_max)
    row_total = jnp.sum(raised, axis=-1, keepdims=True)
    attn_prob = raised / row_total
    log_total = row_max + jnp.log(row_total)
    context = jnp.einsum(
        "bhqk,bkhd->bqhd",
        attn_prob.astype(jnp.bfloat16),
        value_all,
        preferred_element_type=jnp.float32,
    )
    context = context.astype(jnp.bfloat16).reshape(row_count, local_width)
    attended = lax.psum(contract(context, proj_full, 1, 1), "tp") + proj_bias.astype(jnp.float32)
    middle = entering + attended
    normed_two = layer_norm(middle, gain_two, shift_two).astype(jnp.bfloat16)
    pre_act = (
        jnp.dot(normed_two, up_full, preferred_element_type=jnp.float32)
        + up_bias.astype(jnp.float32)[:, 0]
    )
    active = jax.nn.gelu(pre_act, approximate=False).astype(jnp.bfloat16)
    branch = lax.psum(contract(active, down_full, 1, 1).astype(jnp.bfloat16), "tp").astype(
        jnp.float32
    ) + down_bias.astype(jnp.float32)
    result = middle + branch
    output = result.astype(jnp.bfloat16).reshape(images, half_slots, D)
    square_sums = jnp.stack(
        [
            jnp.sum(row_valid * stat_term * stat_term)
            for stat_term in (entering, attended, middle, branch, result)
        ]
    )
    valid_count = jnp.sum(is_valid)
    total_squares, total_count = lax.psum((square_sums, valid_count), ("fsdp", "ctx"))
    rms = jnp.sqrt(total_squares / (total_count * D))
    grad_low = grad_out.reshape(row_count, D)
    grad_res = grad_low.astype(jnp.float32)
    grad_down_bias = jnp.sum(grad_res, axis=0)
    grad_down = contract(grad_low, active, 0, 0)
    grad_active = jnp.dot(grad_low, down_full, preferred_element_type=jnp.float32)
    _, gelu_pull = jax.vjp(partial(jax.nn.gelu, approximate=False), pre_act)
    grad_pre = gelu_pull(grad_active)[0].astype(jnp.bfloat16)
    grad_up_bias = jnp.sum(grad_pre.astype(jnp.float32), axis=0)[:, None]
    grad_up = contract(normed_two, grad_pre, 0, 0)
    grad_normed_two = lax.psum(contract(grad_pre, up_full, 1, 1), "tp")
    _, norm_pull_two = jax.vjp(layer_norm, middle, gain_two, shift_two)
    grad_mid_part, grad_gain_two, grad_shift_two = norm_pull_two(grad_normed_two)
    grad_middle = grad_res + grad_mid_part
    grad_att = grad_middle.astype(jnp.bfloat16)
    grad_proj_bias = jnp.sum(grad_att.astype(jnp.float32), axis=0)
    grad_proj = contract(grad_att, context, 0, 0)
    grad_context = (
        jnp.dot(grad_att, proj_full, preferred_element_type=jnp.float32)
        .astype(jnp.bfloat16)
        .reshape(head_shape)
    )
    scores_again = attn_scores(query_heads, key_all, key_valid)
    prob_again = jnp.exp(scores_again - log_total)
    grad_prob = jnp.einsum(
        "bqhd,bkhd->bhqk", grad_context, value_all, preferred_element_type=jnp.float32
    )
    grad_scores = (
        prob_again * (grad_prob - jnp.sum(prob_again * grad_prob, axis=-1, keepdims=True))
    ).astype(jnp.bfloat16)
    score_scale = HD ** (-0.5)
    grad_query = (
        jnp.einsum("bhqk,bkhd->bqhd", grad_scores, key_all, preferred_element_type=jnp.float32)
        * score_scale
    )
    grad_query = grad_query.astype(jnp.bfloat16).reshape(row_count, local_width)
    key_terms = (
        jnp.einsum("bhqk,bqhd->bkhd", grad_scores, query_heads, preferred_element_type=jnp.float32)
        * score_scale
    )
    value_terms = jnp.einsum(
        "bhqk,bqhd->bkhd",
        prob_again.astype(jnp.bfloat16),
        grad_context,
        preferred_element_type=jnp.float32,
    )
    key_summed, value_summed = (
        lax.psum_scatter(key_terms, "ctx", scatter_dimension=1, tiled=True),
        lax.psum_scatter(value_terms, "ctx", scatter_dimension=1, tiled=True),
    )
    grad_key = key_summed.astype(jnp.bfloat16).reshape(row_count, local_width)
    grad_value = value_summed.astype(jnp.bfloat16).reshape(row_count, local_width)
    grad_packed = jnp.stack([grad_query, grad_key, grad_value], axis=1).reshape(
        row_count, 3 * local_width
    )
    grad_qkv = contract(normed, grad_packed, 0, 0).reshape(D, 3, local_width)
    grad_qv_bias = jnp.concatenate(
        [
            jnp.sum(grad_query.astype(jnp.float32), axis=0),
            jnp.sum(grad_value.astype(jnp.float32), axis=0),
        ]
    )[:, None]
    grad_normed = lax.psum(contract(grad_packed, qkv_flat, 1, 1).astype(jnp.bfloat16), "tp").astype(
        jnp.float32
    )
    _, norm_pull_one = jax.vjp(layer_norm, entering, gain_one, shift_one)
    grad_enter_part, grad_gain_one, grad_shift_one = norm_pull_one(grad_normed)
    grad_inputs = ((grad_middle + grad_enter_part) * row_valid).reshape(images, half_slots, D)
    summed = (
        lax.psum_scatter(grad_gain_one, ("fsdp", "ctx"), scatter_dimension=0, tiled=True),
        lax.psum_scatter(grad_shift_one, ("fsdp", "ctx"), scatter_dimension=0, tiled=True),
        lax.psum_scatter(grad_qkv, ("fsdp", "ctx"), scatter_dimension=0, tiled=True),
        lax.psum_scatter(grad_qv_bias, ("fsdp", "ctx"), scatter_dimension=0, tiled=True),
        lax.psum_scatter(grad_proj, ("fsdp", "ctx"), scatter_dimension=0, tiled=True),
        lax.psum_scatter(grad_proj_bias, ("fsdp", "ctx"), scatter_dimension=0, tiled=True),
        lax.psum_scatter(grad_gain_two, ("fsdp", "ctx"), scatter_dimension=0, tiled=True),
        lax.psum_scatter(grad_shift_two, ("fsdp", "ctx"), scatter_dimension=0, tiled=True),
        lax.psum_scatter(grad_up, ("fsdp", "ctx"), scatter_dimension=0, tiled=True),
        lax.psum_scatter(grad_up_bias, ("fsdp", "ctx"), scatter_dimension=0, tiled=True),
        lax.psum_scatter(grad_down, ("fsdp", "ctx"), scatter_dimension=0, tiled=True),
        lax.psum_scatter(grad_down_bias, ("fsdp", "ctx"), scatter_dimension=0, tiled=True),
    )
    return (
        output,
        grad_inputs,
        summed[0],
        summed[1],
        summed[2],
        summed[3],
        summed[4],
        summed[5],
        summed[6],
        summed[7],
        summed[8],
        summed[9],
        summed[10],
        summed[11],
        rms,
    )


def solution(mesh):
    in_specs = (
        P("fsdp", "ctx", None),
        P("fsdp"),
        P("fsdp", "ctx", None),
        P(("fsdp", "ctx")),
        P(("fsdp", "ctx")),
        P(("fsdp", "ctx"), None, "tp"),
        P(("fsdp", "ctx"), "tp"),
        P(("fsdp", "ctx"), "tp"),
        P(("fsdp", "ctx")),
        P(("fsdp", "ctx")),
        P(("fsdp", "ctx")),
        P(("fsdp", "ctx"), "tp"),
        P(("fsdp", "ctx"), "tp"),
        P(("fsdp", "ctx"), "tp"),
        P(("fsdp", "ctx")),
    )
    out_specs = (
        P("fsdp", "ctx", None),
        P("fsdp", "ctx", None),
        P(("fsdp", "ctx")),
        P(("fsdp", "ctx")),
        P(("fsdp", "ctx"), None, "tp"),
        P(("fsdp", "ctx"), "tp"),
        P(("fsdp", "ctx"), "tp"),
        P(("fsdp", "ctx")),
        P(("fsdp", "ctx")),
        P(("fsdp", "ctx")),
        P(("fsdp", "ctx"), "tp"),
        P(("fsdp", "ctx"), "tp"),
        P(("fsdp", "ctx"), "tp"),
        P(("fsdp", "ctx")),
        P(),
    )
    return jax.shard_map(body, mesh=mesh, in_specs=in_specs, out_specs=out_specs, check_vma=False)
```

profile of v0, /device:TPU:0, one launch (start us, length us, event | category | flops | bytes accessed | tf_op | source)
XLA Modules:
  0.0 852.9 jit_solution(4844973030946835387)
XLA Ops:
  16.6 63.5 %all-reduce.14 = (bf16[1024]{0:T(1024)(128)(2,1)S(1)}, bf16[1024]{0:T(1024)(128)(2,1)S(1)}, bf16[1024]{0:T(1024)(128)(2,1)S(1)}, bf16[1024]{0:T(1024)(128)(2,1)S...) all-reduce(bf16[1024]{0:T(1024)(128)(2,1)S(1)} %dynamic-update-slic, ...), channel_id=1, replica_groups=mesh['fsdp'=8,'ctx'=2,'tp'=2] {'fsdp','ctx'}, use_global_device_ids=true, to_apply=%add.2 | all-reduce | flops 7168 | bytes 28672
  103.3 17.4 %all_gather.53 = bf16[2048,1]{0,1:T(2,128)(2,1)S(1)} all-gather(bf16[128,1]{0,1:T(2,128)(2,1)S(1)} %copy-done.27), channel_id=1, replica_groups=mesh['fsdp'=8,'ctx'=2,'tp'=2] {'fsdp','ctx'}, dimensions={0}, use_global_device_ids=true | all-gather | bytes 4352 | tf_op jit(solution)/shard_map/all_gather | solution.py:60
  120.8 10.3 %all-reduce.20.cloned.1.call-done = f32[160,1024]{1,0:T(8,128)} async-done(((f32[160,1024]{1,0:T(8,128)}), f32[160,1024]{1,0:T(8,128)}) %all-reduce.20.cloned.1.call-update) | async-done | bytes 655376 | tf_op jit(solution)/shard_map/psum | solution.py:120
  132.6 50.9 %all-gather.9.cloned.1.call-done = bf16[1024,2048]{1,0:T(8,128)(2,1)} async-done(((bf16[64,2048]{1,0:T(8,128)(2,1)}), bf16[1024,2048]{1,0:T(8,128)(2,1)}) %all-gather.9.cloned.1.call-update) | async-done | bytes 4194320 | tf_op jit(solution)/shard_map/all_gather | solution.py:59
  183.5 7.1 multiply_convert_fusion.1
  190.6 43.8 %all-gather.11.cloned.1.call-done = bf16[1024,2048]{1,0:T(8,128)(2,1)} async-done(((bf16[64,2048]{1,0:T(8,128)(2,1)}), bf16[1024,2048]{1,0:T(8,128)(2,1)}) %all-gather.11.cloned.1.call-update) | async-done | bytes 4194320 | tf_op jit(solution)/shard_map/all_gather | solution.py:61
  234.4 4.7 convolution_convert_fusion
  239.1 7.2 convert_reduce_fusion
  249.9 12.2 %all-reduce.22.cloned.1.call-done = bf16[160,1024]{1,0:T(8,128)(2,1)} async-done(((bf16[160,1024]{1,0:T(8,128)(2,1)}), bf16[160,1024]{1,0:T(8,128)(2,1)}) %all-reduce.22.cloned.1.call-update) | async-done | bytes 327696 | tf_op jit(solution)/shard_map/psum | solution.py:128
  262.1 33.8 %all-reduce.24.cloned.1.call-done = f32[160,1024]{1,0:T(8,128)} async-done(((f32[160,1024]{1,0:T(8,128)}), f32[160,1024]{1,0:T(8,128)}) %all-reduce.24.cloned.1.call-update) | async-done | bytes 655376 | tf_op jit(solution)/shard_map/psum | solution.py:151
  296.0 3.4 fusion.36
  322.3 8.1 reduce-scatter.25.cloned.1.call-done
  333.3 3.9 fusion.11
  339.1 3.9 fusion.38
  344.1 4.6 fusion.62
  349.9 4.5 convolution_bitcast_fusion
  354.4 9.1 %copy.92 = f32[1024,2048]{1,0:T(8,128)} copy(f32[1024,2048]{0,1:T(8,128)} %convolution_bitcast_fusion) | data formatting | bytes 16777216
  364.9 27.8 %reduce-scatter.31.cloned.1.call-done = f32[128,1]{1,0:T(8,128)} async-done(((f32[2048,1]{1,0:T(8,128)}), f32[128,1]{1,0:T(8,128)}) %reduce-scatter.31.cloned.1.call-update) | async-done | bytes 528
  394.1 57.4 %reduce-scatter.29.cloned.1.call-done = f32[64,1]{1,0:T(8,128)} async-done(((f32[1024,1]{1,0:T(8,128)}), f32[64,1]{1,0:T(8,128)}) %reduce-scatter.29.cloned.1.call-update) | async-done | bytes 272
  452.8 24.2 %all-reduce.26.cloned.1.call-done = bf16[160,1024]{1,0:T(8,128)(2,1)} async-done(((bf16[160,1024]{1,0:T(8,128)(2,1)}), bf16[160,1024]{1,0:T(8,128)(2,1)}) %all-reduce.26.cloned.1.call-update) | async-done | bytes 327696 | tf_op jit(solution)/shard_map/psum | solution.py:203
  485.2 61.3 %all-reduce.13 = (f32[1024]{0:T(1024)S(1)}, f32[1024]{0:T(1024)S(1)}, f32[1024]{0:T(1024)S(1)}, f32[1024]{0:T(1024)S(1)}, f32[1024]{0:T(1024)S(1)}, /*index=5*/f32[1024]{0:T(1024)S(1)}, f32[5]{0:T(128)S(1)}, f32[]{:T(128)}) all-reduce(f32[1024]{0:T(1024)S(1)} %get-tuple-element.77, ...), channel_id=4, replica_groups=mesh['fsdp'=8,'ctx'=2,'tp'=2] {'fsdp','ctx'}, use_global_device_ids=true, to_apply=%region_18.19.clone | all-reduce | flops 6150 | bytes 49200
  551.2 80.4 %reduce-scatter.19.cloned.1.call-done = f32[64,3,512]{2,0,1:T(8,128)} async-done(((f32[1024,3,512]{2,0,1:T(8,128)}), f32[64,3,512]{2,0,1:T(8,128)}) %reduce-scatter.19.cloned.1.call-update) | async-done | bytes 393232 | tf_op jit(solution)/shard_map/reduce_scatter | solution.py:212
  631.7 107.0 %reduce-scatter.23.cloned.1.call-done = f32[64,2048]{1,0:T(8,128)} async-done(((f32[1024,2048]{1,0:T(8,128)}), f32[64,2048]{1,0:T(8,128)}) %reduce-scatter.23.cloned.1.call-update) | async-done | bytes 524304 | tf_op jit(solution)/shard_map/reduce_scatter | solution.py:218
  738.7 107.6 %reduce-scatter.33.cloned.1.call-done = f32[64,2048]{1,0:T(8,128)} async-done(((f32[1024,2048]{1,0:T(8,128)}), f32[64,2048]{1,0:T(8,128)}) %reduce-scatter.33.cloned.1.call-update) | async-done | bytes 524304
  (192 shorter events, 81.5 us)
Async XLA Ops:
  7.2 76.6 %all-gather.5.cloned.1.call-start = ((), (), s32[]{:S(2)}) async-start(), calls=%async_computation.8 | async-start | bytes 3342336 | tf_op jit(solution)/shard_map/all_gather | solution.py:53
  7.9 91.4 %all-gather.7.cloned.1.call-start = ((), (), s32[]{:S(2)}) async-start(), calls=%async_computation.9 | async-start | bytes 1114112 | tf_op jit(solution)/shard_map/all_gather | solution.py:55
  8.7 122.4 %all-reduce.20.cloned.1.call-start = ((), (), s32[]{:S(2)}) async-start(), calls=%async_computation.10 | async-start | bytes 1310720 | tf_op jit(solution)/shard_map/psum | solution.py:120
  99.4 3.9 copy-start.27
  102.1 81.4 %all-gather.9.cloned.1.call-start = ((), (), s32[]{:S(2)}) async-start(), calls=%async_computation.11 | async-start | bytes 4456448 | tf_op jit(solution)/shard_map/all_gather | solution.py:59
  102.6 131.8 %all-gather.11.cloned.1.call-start = ((), (), s32[]{:S(2)}) async-start(), calls=%async_computation.12 | async-start | bytes 4456448 | tf_op jit(solution)/shard_map/all_gather | solution.py:61
  103.2 158.9 %all-reduce.22.cloned.1.call-start = ((), (), s32[]{:S(2)}) async-start(), calls=%async_computation.13 | async-start | bytes 655360 | tf_op jit(solution)/shard_map/psum | solution.py:128
  239.1 56.9 %all-reduce.24.cloned.1.call-start = ((), (), s32[]{:S(2)}) async-start(), calls=%async_computation.14 | async-start | bytes 1310720 | tf_op jit(solution)/shard_map/psum | solution.py:151
  239.1 8.1 copy-start.5
  249.6 71.1 %reduce-scatter.27.cloned.1.call-start = ((), (), s32[]{:S(2)}) async-start(), calls=%async_computation.20 | async-start | bytes 983040
  310.8 19.6 %reduce-scatter.25.cloned.1.call-start = ((), (), s32[]{:S(2)}) async-start(), calls=%async_computation.19 | async-start | bytes 983040
  318.3 74.3 %reduce-scatter.31.cloned.1.call-start = ((), (), s32[]{:S(2)}) async-start(), calls=%async_computation.22 | async-start | bytes 1114112
  319.8 131.7 %reduce-scatter.29.cloned.1.call-start = ((), (), s32[]{:S(2)}) async-start(), calls=%async_computation.21 | async-start | bytes 557056
  333.2 4.0 copy-start.10
  333.2 4.0 copy-start.19
  333.2 143.8 %all-reduce.26.cloned.1.call-start = ((), (), s32[]{:S(2)}) async-start(), calls=%async_computation.15 | async-start | bytes 655360 | tf_op jit(solution)/shard_map/psum | solution.py:203
  337.2 214.1 %reduce-scatter.21.cloned.1.call-start = ((), (), s32[]{:S(2)}) async-start(), calls=%async_computation.17 | async-start | bytes 2228224 | tf_op jit(solution)/shard_map/reduce_scatter | solution.py:214
  339.1 292.6 %reduce-scatter.19.cloned.1.call-start = ((), (), s32[]{:S(2)}) async-start(), calls=%async_computation.16 | async-start | bytes 6684672 | tf_op jit(solution)/shard_map/reduce_scatter | solution.py:212
  343.0 395.7 %reduce-scatter.23.cloned.1.call-start = ((), (), s32[]{:S(2)}) async-start(), calls=%async_computation.18 | async-start | bytes 8912896 | tf_op jit(solution)/shard_map/reduce_scatter | solution.py:218
  348.7 497.6 %reduce-scatter.33.cloned.1.call-start = ((), (), s32[]{:S(2)}) async-start(), calls=%async_computation.23 | async-start | bytes 8912896
  363.5 119.0 %copy-start.23 = (f32[160]{0:T(256)S(1)}, f32[160]{0:T(256)}, u32[]{:S(2)}) copy-start(f32[160]{0:T(256)} %copy-done.22) | copy-start | bytes 1924
  363.5 120.4 %copy-start.4 = (f32[160,1024]{1,0:T(8,128)S(1)}, f32[160,1024]{1,0:T(8,128)}, u32[]{:S(2)}) copy-start(f32[160,1024]{1,0:T(8,128)} %copy-done.3) | copy-start | bytes 1966084
  363.5 120.4 %copy-start.25 = (f32[160]{0:T(256)S(1)}, f32[160]{0:T(256)}, u32[]{:S(2)}) copy-start(f32[160]{0:T(256)} %copy-done.24) | copy-start | bytes 1924
  477.0 6.9 copy-start.8
  (20 other events, 30.0 us)
Sparse Core Ops, SparseCore 0:
  10.2 48.3 all-gather.4
  60.7 36.5 all-gather.6
  102.2 28.8 all-reduce.19
  133.1 50.3 all-gather.8
  185.5 48.8 all-gather.10
  239.2 22.8 all-reduce.21
  264.4 31.5 all-reduce.23
  310.9 8.0 reduce-scatter.26
  321.3 9.1 reduce-scatter.24
  333.9 58.6 reduce-scatter.30
  396.2 55.2 reduce-scatter.28
  453.6 23.3 all-reduce.25
  481.4 61.9 reduce-scatter.20
  547.7 83.9 reduce-scatter.18
  636.1 102.5 reduce-scatter.22
  743.2 103.0 reduce-scatter.32
where the time goes:
time: 854 us; the launch traced here: 853 us
  waiting for transfers between devices  566 us (66%)
  blocking collectives  147 us (17%)
  local copies, waits for them, and re-layouts  52.8 us (6%)
  matrix products  52.7 us (6%)
  between operations  17.2 us (2%)
  other arithmetic  15.9 us (2%)
    unnamed x21, waiting for transfers between devices  204 us
    unnamed x2, blocking collectives  125 us
    reduce_scatter x1, waiting for transfers between devices, body(): lax.psum_scatter(grad_up, ('fsdp', 'ctx'), scatter_dimension=0, tiled=True)  107 us
    reduce_scatter x1, waiting for transfers between devices, body(): lax.psum_scatter(grad_qkv, ('fsdp', 'ctx'), scatter_dimension=0, tiled=True)  80.4 us
    all_gather x1, waiting for transfers between devices, body(): lax.all_gather(w_up, ('fsdp', 'ctx'), axis=0, tiled=True)  50.9 us
    all_gather x1, waiting for transfers between devices, body(): lax.all_gather(w_down, ('fsdp', 'ctx'), axis=0, tiled=True)  43.8 us
    unnamed x90, local copies, waits for them, and re-layouts  41.7 us
    psum x1, waiting for transfers between devices, body(): grad_normed_two = lax.psum(contract(grad_pre, up_full, 1, 1), 'tp')  33.8 us
  transfers between devices with their start and end apart: 16, of which 12 were waited for; matrix products, arithmetic and copies ran while one was open for 11% of the time, Pallas kernels for 0%

commit v1 on v0

--- a/solution.py
+++ b/solution.py
@@ -148,7 +148,8 @@
     grad_pre = gelu_pull(grad_active)[0].astype(jnp.bfloat16)
     grad_up_bias = jnp.sum(grad_pre.astype(jnp.float32), axis=0)[:, None]
     grad_up = contract(normed_two, grad_pre, 0, 0)
-    grad_normed_two = lax.psum(contract(grad_pre, up_full, 1, 1), "tp")
+    array_here = contract(grad_pre, up_full, 1, 1)
+    grad_normed_two = jnp.sum(jax.lax.all_gather(array_here, "tp"), axis=0)
     _, norm_pull_two = jax.vjp(layer_norm, middle, gain_two, shift_two)
     grad_mid_part, grad_gain_two, grad_shift_two = norm_pull_two(grad_normed_two)
     grad_middle = grad_res + grad_mid_part

time: 854 us -> 853 us (level)
    psum x1 -> x0, waiting for transfers between devices: 33.8 us -> none  [body(): grad_normed_two = lax.psum(contract(grad_pre, up_full, 1, 1), 'tp')]
    all_gather x0 -> x1, waiting for transfers between devices: none -> 17.9 us  [body(): grad_normed_two = jnp.sum(jax.lax.all_gather(array_here, 'tp'), axis=0)]
    psum x1, waiting for transfers between devices: 12.2 us -> 24.9 us  [body(): lax.psum(contract(active, down_full, 1, 1).astype(jnp.bfloat16), 'tp')]
    unnamed x90 -> x96, local copies, waits for them, and re-layouts: 41.7 us -> 42.3 us
where the time goes in v1:
time: 853 us; the launch traced here: 852 us
  waiting for transfers between devices  563 us (66%)
  blocking collectives  148 us (17%)
  local copies, waits for them, and re-layouts  52.8 us (6%)
  matrix products  51.7 us (6%)
  other arithmetic  18.2 us (2%)
  between operations  17.2 us (2%)
    unnamed x21, waiting for transfers between devices  203 us
    unnamed x2, blocking collectives  125 us
    reduce_scatter x1, waiting for transfers between devices, body(): lax.psum_scatter(grad_up, ('fsdp', 'ctx'), scatter_dimension=0, tiled=True)  107 us
    reduce_scatter x1, waiting for transfers between devices, body(): lax.psum_scatter(grad_qkv, ('fsdp', 'ctx'), scatter_dimension=0, tiled=True)  80.4 us
    all_gather x1, waiting for transfers between devices, body(): lax.all_gather(w_up, ('fsdp', 'ctx'), axis=0, tiled=True)  50.9 us
    all_gather x1, waiting for transfers between devices, body(): lax.all_gather(w_down, ('fsdp', 'ctx'), axis=0, tiled=True)  43.8 us
    unnamed x96, local copies, waits for them, and re-layouts  42.3 us
    dot_general x8, matrix products, contract(): lax.dot_general(left, right, (((left_dim,), (right_dim,)), ((), ())), pre...  28.3 us
  transfers between devices with their start and end apart: 16, of which 12 were waited for; matrix products, arithmetic and copies ran while one was open for 11% of the time, Pallas kernels for 0%

profile of v1, /device:TPU:0, one launch (start us, length us, event | category | flops | bytes accessed | tf_op | source)
XLA Modules:
  0.0 851.6 jit_solution(8293648787805773083)
XLA Ops:
  19.7 63.4 %all-reduce.14 = (bf16[1024]{0:T(1024)(128)(2,1)S(1)}, bf16[1024]{0:T(1024)(128)(2,1)S(1)}, bf16[1024]{0:T(1024)(128)(2,1)S(1)}, bf16[1024]{0:T(1024)(128)(2,1)S...) all-reduce(bf16[1024]{0:T(1024)(128)(2,1)S(1)} %dynamic-update-slic, ...), channel_id=1, replica_groups=mesh['fsdp'=8,'ctx'=2,'tp'=2] {'fsdp','ctx'}, use_global_device_ids=true, to_apply=%add.2 | all-reduce | flops 7168 | bytes 28672
  102.4 18.4 %all_gather.59 = bf16[2048,1]{0,1:T(2,128)(2,1)S(1)} all-gather(bf16[128,1]{0,1:T(2,128)(2,1)S(1)} %copy-done.30), channel_id=1, replica_groups=mesh['fsdp'=8,'ctx'=2,'tp'=2] {'fsdp','ctx'}, dimensions={0}, use_global_device_ids=true | all-gather | bytes 4352 | tf_op jit(solution)/shard_map/all_gather | solution.py:60
  120.8 9.9 %all-reduce.19.cloned.1.call-done = f32[160,1024]{1,0:T(8,128)} async-done(((f32[160,1024]{1,0:T(8,128)}), f32[160,1024]{1,0:T(8,128)}) %all-reduce.19.cloned.1.call-update) | async-done | bytes 655376 | tf_op jit(solution)/shard_map/psum | solution.py:120
  132.3 50.9 %all-gather.11.cloned.1.call-done = bf16[1024,2048]{1,0:T(8,128)(2,1)} async-done(((bf16[64,2048]{1,0:T(8,128)(2,1)}), bf16[1024,2048]{1,0:T(8,128)(2,1)}) %all-gather.11.cloned.1.call-update) | async-done | bytes 4194320 | tf_op jit(solution)/shard_map/all_gather | solution.py:59
  183.2 7.1 multiply_convert_fusion.1
  190.3 43.8 %all-gather.13.cloned.1.call-done = bf16[1024,2048]{1,0:T(8,128)(2,1)} async-done(((bf16[64,2048]{1,0:T(8,128)(2,1)}), bf16[1024,2048]{1,0:T(8,128)(2,1)}) %all-gather.13.cloned.1.call-update) | async-done | bytes 4194320 | tf_op jit(solution)/shard_map/all_gather | solution.py:61
  234.1 7.2 convert_reduce_fusion
  244.6 4.7 convolution_convert_fusion
  249.6 17.9 %all-gather.15.cloned.1.call-done = f32[320,1024]{1,0:T(8,128)} async-done(((f32[160,1024]{1,0:T(8,128)}), f32[320,1024]{1,0:T(8,128)}) %all-gather.15.cloned.1.call-update) | async-done | bytes 1310736 | tf_op jit(solution)/shard_map/all_gather | solution.py:152
  269.8 24.9 %all-reduce.21.cloned.1.call-done = bf16[160,1024]{1,0:T(8,128)(2,1)} async-done(((bf16[160,1024]{1,0:T(8,128)(2,1)}), bf16[160,1024]{1,0:T(8,128)(2,1)}) %all-reduce.21.cloned.1.call-update) | async-done | bytes 327696 | tf_op jit(solution)/shard_map/psum | solution.py:128
  322.2 6.9 reduce-scatter.25.cloned.1.call-done
  330.8 3.8 fusion.11
  336.6 3.9 fusion.38
  341.5 4.6 fusion.62
  347.3 4.5 convolution_bitcast_fusion
  351.9 9.1 %copy.92 = f32[1024,2048]{1,0:T(8,128)} copy(f32[1024,2048]{0,1:T(8,128)} %convolution_bitcast_fusion) | data formatting | bytes 16777216
  362.4 29.0 %reduce-scatter.31.cloned.1.call-done = f32[128,1]{1,0:T(8,128)} async-done(((f32[2048,1]{1,0:T(8,128)}), f32[128,1]{1,0:T(8,128)}) %reduce-scatter.31.cloned.1.call-update) | async-done | bytes 528
  392.9 57.3 %reduce-scatter.29.cloned.1.call-done = f32[64,1]{1,0:T(8,128)} async-done(((f32[1024,1]{1,0:T(8,128)}), f32[64,1]{1,0:T(8,128)}) %reduce-scatter.29.cloned.1.call-update) | async-done | bytes 272
  451.5 24.2 %all-reduce.23.cloned.1.call-done = bf16[160,1024]{1,0:T(8,128)(2,1)} async-done(((bf16[160,1024]{1,0:T(8,128)(2,1)}), bf16[160,1024]{1,0:T(8,128)(2,1)}) %all-reduce.23.cloned.1.call-update) | async-done | bytes 327696 | tf_op jit(solution)/shard_map/psum | solution.py:204
  477.8 3.3 stack.27
  483.8 61.3 %all-reduce.13 = (f32[1024]{0:T(1024)S(1)}, f32[1024]{0:T(1024)S(1)}, f32[1024]{0:T(1024)S(1)}, f32[1024]{0:T(1024)S(1)}, f32[1024]{0:T(1024)S(1)}, /*index=5*/f32[1024]{0:T(1024)S(1)}, f32[5]{0:T(128)S(1)}, f32[]{:T(128)}) all-reduce(f32[1024]{0:T(1024)S(1)} %get-tuple-element.77, ...), channel_id=5, replica_groups=mesh['fsdp'=8,'ctx'=2,'tp'=2] {'fsdp','ctx'}, use_global_device_ids=true, to_apply=%region_18.19.clone | all-reduce | flops 6150 | bytes 49200
  549.9 80.4 %reduce-scatter.19.cloned.1.call-done = f32[64,3,512]{2,0,1:T(8,128)} async-done(((f32[1024,3,512]{2,0,1:T(8,128)}), f32[64,3,512]{2,0,1:T(8,128)}) %reduce-scatter.19.cloned.1.call-update) | async-done | bytes 393232 | tf_op jit(solution)/shard_map/reduce_scatter | solution.py:213
  630.3 107.2 %reduce-scatter.23.cloned.1.call-done = f32[64,2048]{1,0:T(8,128)} async-done(((f32[1024,2048]{1,0:T(8,128)}), f32[64,2048]{1,0:T(8,128)}) %reduce-scatter.23.cloned.1.call-update) | async-done | bytes 524304 | tf_op jit(solution)/shard_map/reduce_scatter | solution.py:219
  737.4 107.6 %reduce-scatter.33.cloned.1.call-done = f32[64,2048]{1,0:T(8,128)} async-done(((f32[1024,2048]{1,0:T(8,128)}), f32[64,2048]{1,0:T(8,128)}) %reduce-scatter.33.cloned.1.call-update) | async-done | bytes 524304
  (200 shorter events, 82.9 us)
Async XLA Ops:
  7.2 76.1 %all-gather.7.cloned.1.call-start = ((), (), s32[]{:S(2)}) async-start(), calls=%async_computation.8 | async-start | bytes 3342336 | tf_op jit(solution)/shard_map/all_gather | solution.py:53
  7.9 90.5 %all-gather.9.cloned.1.call-start = ((), (), s32[]{:S(2)}) async-start(), calls=%async_computation.9 | async-start | bytes 1114112 | tf_op jit(solution)/shard_map/all_gather | solution.py:55
  8.7 122.1 %all-reduce.19.cloned.1.call-start = ((), (), s32[]{:S(2)}) async-start(), calls=%async_computation.10 | async-start | bytes 1310720 | tf_op jit(solution)/shard_map/psum | solution.py:120
  11.8 71.4 %copy-start.25 = (f32[160]{0:T(256)}, f32[160]{0:T(256)S(1)}, u32[]{:S(2)}) copy-start(f32[160]{0:T(256)S(1)} %fusion.25) | copy-start | bytes 1924
  101.2 82.0 %all-gather.11.cloned.1.call-start = ((), (), s32[]{:S(2)}) async-start(), calls=%async_computation.11 | async-start | bytes 4456448 | tf_op jit(solution)/shard_map/all_gather | solution.py:59
  101.7 132.4 %all-gather.13.cloned.1.call-start = ((), (), s32[]{:S(2)}) async-start(), calls=%async_computation.12 | async-start | bytes 4456448 | tf_op jit(solution)/shard_map/all_gather | solution.py:61
  102.3 165.2 %all-gather.15.cloned.1.call-start = ((), (), s32[]{:S(2)}) async-start(), calls=%async_computation.18 | async-start | bytes 1966080 | tf_op jit(solution)/shard_map/all_gather | solution.py:152
  234.1 8.1 copy-start.7
  244.6 50.2 %all-reduce.21.cloned.1.call-start = ((), (), s32[]{:S(2)}) async-start(), calls=%async_computation.13 | async-start | bytes 655360 | tf_op jit(solution)/shard_map/psum | solution.py:128
  249.3 70.0 %reduce-scatter.27.cloned.1.call-start = ((), (), s32[]{:S(2)}) async-start(), calls=%async_computation.20 | async-start | bytes 983040
  309.5 19.6 %reduce-scatter.25.cloned.1.call-start = ((), (), s32[]{:S(2)}) async-start(), calls=%async_computation.19 | async-start | bytes 983040
  317.0 74.3 %reduce-scatter.31.cloned.1.call-start = ((), (), s32[]{:S(2)}) async-start(), calls=%async_computation.22 | async-start | bytes 1114112
  318.4 131.7 %reduce-scatter.29.cloned.1.call-start = ((), (), s32[]{:S(2)}) async-start(), calls=%async_computation.21 | async-start | bytes 557056
  330.7 4.0 copy-start.14
  330.7 144.9 %all-reduce.23.cloned.1.call-start = ((), (), s32[]{:S(2)}) async-start(), calls=%async_computation.14 | async-start | bytes 655360 | tf_op jit(solution)/shard_map/psum | solution.py:204
  334.6 215.2 %reduce-scatter.21.cloned.1.call-start = ((), (), s32[]{:S(2)}) async-start(), calls=%async_computation.16 | async-start | bytes 2228224 | tf_op jit(solution)/shard_map/reduce_scatter | solution.py:215
  336.5 293.7 %reduce-scatter.19.cloned.1.call-start = ((), (), s32[]{:S(2)}) async-start(), calls=%async_computation.15 | async-start | bytes 6684672 | tf_op jit(solution)/shard_map/reduce_scatter | solution.py:213
  340.5 397.0 %reduce-scatter.23.cloned.1.call-start = ((), (), s32[]{:S(2)}) async-start(), calls=%async_computation.17 | async-start | bytes 8912896 | tf_op jit(solution)/shard_map/reduce_scatter | solution.py:219
  346.2 498.9 %reduce-scatter.33.cloned.1.call-start = ((), (), s32[]{:S(2)}) async-start(), calls=%async_computation.23 | async-start | bytes 8912896
  361.0 31.8 %copy-start.6 = (f32[320,1024]{1,0:T(8,128)S(1)}, f32[320,1024]{1,0:T(8,128)}, u32[]{:S(2)}) copy-start(f32[320,1024]{1,0:T(8,128)} %all-gather.15.cloned.1.call-done) | copy-start | bytes 3932164
  361.0 120.1 %copy-start.26 = (f32[160]{0:T(256)S(1)}, f32[160]{0:T(256)}, u32[]{:S(2)}) copy-start(f32[160]{0:T(256)} %copy-done.25) | copy-start | bytes 1924
  392.8 89.8 %copy-start.5 = (f32[160,1024]{1,0:T(8,128)S(1)}, f32[160,1024]{1,0:T(8,128)}, u32[]{:S(2)}) copy-start(f32[160,1024]{1,0:T(8,128)} %copy-done.4) | copy-start | bytes 1966084
  392.8 89.8 %copy-start.28 = (f32[160]{0:T(256)S(1)}, f32[160]{0:T(256)}, u32[]{:S(2)}) copy-start(f32[160]{0:T(256)} %copy-done.27) | copy-start | bytes 1924
  475.7 6.9 copy-start.12
  (23 other events, 40.7 us)
Sparse Core Ops, SparseCore 0:
  10.2 48.6 all-gather.6
  61.0 36.2 all-gather.8
  101.3 29.4 all-reduce.18
  132.7 50.3 all-gather.10
  185.2 48.8 all-gather.12
  244.7 22.7 all-gather.14
  270.3 24.3 all-reduce.20
  309.6 8.0 reduce-scatter.26
  319.9 9.1 reduce-scatter.24
  332.6 58.6 reduce-scatter.30
  394.9 55.1 reduce-scatter.28
  452.3 23.3 all-reduce.22
  480.0 61.9 reduce-scatter.20
  546.3 83.9 reduce-scatter.18
  634.7 102.6 reduce-scatter.22
  741.9 103.0 reduce-scatter.32
